TPU v7x, 32 devices: a whole 2x2x4 slice. The times are simulated.
32 devices in a mesh: cell: 16 (over z, y, x), win: 2 (over core).
Axes of the slice: x: 2, y: 2, z: 4, core: 2. Of those that a mesh axis runs over, the one named last changes fastest.
Arguments:
- anomalies: bfloat16 [256, 60, 8192], P('win', None, 'cell'), may hold values from -6 to 6
- eofs: bfloat16 [100, 60, 8192], P('win', None, 'cell'), may hold values from -0.015625 to 0.015625
- cell_area: float32 [8192], P('cell'), may hold values from 0.5 to 2
- levels: int32 [8192], P('cell'), may hold values from 1 to 60
- counts: int32 [16], replicated, may hold values from 128 to 512, as said below
Outputs:
- pcs: float32 [256, 100], P('win')
- regression: float32 [100, 8192], P('win', 'cell')
Inputs may be any that keep to these rules, and one draw needn't show every extreme that they name: `counts`: every entry is at most 512, and some block holds exactly 512 real cells.
All inputs are finite; a program needn't handle non-finite values.
Results may differ from a plain program's by a relative error of at most 0.0049.
Values may be sent and summed in bfloat16 or wider, within the bound.
No kernel may reach another device: no remote copies, remote signals or barrier semaphores. Data moves between devices by JAX's collectives and lax.ppermute only.
A program may use at most 64 MiB of HBM per device.

v0:
```python
import jax
import jax.numpy as jnp
from jax import lax
from jax.sharding import PartitionSpec as P


def shards(anomalies, eofs, cell_area, levels, counts):
    steps_here, depth_count, slots = anomalies.shape
    position = lax.axis_index("cell")
    filled = counts[position]
    live = jnp.arange(slots, dtype=jnp.int32) < filled
    depth = jnp.arange(depth_count, dtype=jnp.int32)[:, None] < levels[None, :]
    mask = (live[None, :] & depth).astype(jnp.float32)
    weighted = (eofs.astype(jnp.float32) * (cell_area[None, :] * mask)[None]).astype(jnp.bfloat16)
    flat_data = anomalies.reshape(steps_here, depth_count * slots)
    piece = lax.all_gather(weighted, "win", axis=0, tiled=True)
    flat_piece = piece.reshape(piece.shape[0], depth_count * slots)
    partial_value = lax.dot_general(
        flat_data, flat_piece, (((1,), (1,)), ((), ())), preferred_element_type=jnp.float32
    )
    pcs = lax.psum(partial_value, "cell")
    column = jnp.sum(anomalies.astype(jnp.float32) * mask[None], axis=1).astype(jnp.bfloat16)
    pcs_rounded = pcs.astype(jnp.bfloat16)
    windows = lax.axis_size("win")
    term = lax.dot_general(
        pcs_rounded, column, (((0,), (0,)), ((), ())), preferred_element_type=jnp.float32
    )
    term = term / jnp.sqrt(jnp.float32(steps_here * windows))
    regression = lax.psum_scatter(term, "win", scatter_dimension=0, tiled=True)
    return (pcs, regression)


def solution(mesh):
    in_specs = (P("win", None, "cell"), P("win", None, "cell"), P("cell"), P("cell"), P())
    out_specs = (P("win", None), P("win", "cell"))
    return jax.shard_map(shards, mesh=mesh, in_specs=in_specs, out_specs=out_specs, check_vma=False)
```

profile of v0, /device:TPU:0, one launch (start us, length us, event | category | flops | bytes accessed | tf_op | source)
XLA Modules:
  0.0 138.4 jit_solution(9140950876646721835)
XLA Ops:
  7.2 0.0 copy-start.1
  7.2 0.0 all-gather.2.cloned.1.call-start
  7.2 1.2 dynamic_slice.3
  8.5 0.6 iota_compare_fusion.1
  9.1 0.7 fusion.9
  9.9 4.6 %multiply_convert_fusion = bf16[50,60,512]{2,1,0:T(8,128)(2,1)} fusion(bf16[50,60,512]{2,1,0:T(8,128)(2,1)} %param.6, f32[60,512]{1,0:T(8,128)S(1)} %fusion.9), kind=kLoop, calls=%fused_computation.1 | loop fusion | flops 4608000 | bytes 6266880 | tf_op jit(solution)/shard_map/convert_element_type | solution.py:14
  14.5 0.0 all-gather.2.cloned.1.call-update
  14.5 0.0 copy-done.1
  14.5 5.0 %multiply_reduce_fusion = bf16[128,512]{1,0:T(8,128)(2,1)S(1)} fusion(bf16[128,60,512]{2,0,1:T(8,128)(2,1)} %param.5, f32[60,512]{1,0:T(8,128)S(1)} %fusion.8), kind=kLoop, calls=%fused_computation | loop fusion | flops 11730944 | bytes 8118272 | tf_op jit(solution)/shard_map/reduce_sum | solution.py:22
  19.5 0.0 copy-start.2
  19.5 15.0 %all-gather.2.cloned.1.call-done = bf16[100,60,512]{2,1,0:T(8,128)(2,1)} async-done(((bf16[50,60,512]{2,1,0:T(8,128)(2,1)}), bf16[100,60,512]{2,1,0:T(8,128)(2,1)}) %all-gather.2.cloned.1.call-update) | async-done | bytes 6144016 | tf_op jit(solution)/shard_map/all_gather | solution.py:16
  34.5 12.3 %fusion.3 = f32[128,100]{0,1:T(8,128)S(1)} fusion(bf16[128,60,512]{2,0,1:T(8,128)(2,1)} %param.5, bf16[100,60,512]{2,1,0:T(8,128)(2,1)} %all-gather.2.cloned.1.call-done), kind=kOutput, calls=%fused_computation.5 | convolution fusion | flops 786432000 | bytes 14059520 | tf_op jit(solution)/shard_map/dot_general | solution.py:18
  46.8 77.1 %psum.7 = f32[128,100]{0,1:T(8,128)S(1)} all-reduce(f32[128,100]{0,1:T(8,128)S(1)} %fusion.3), channel_id=1, replica_groups=mesh['cell'=16,'win'=2] {'cell'}, use_global_device_ids=true, to_apply=%region_0.0 | all-reduce | flops 12800 | bytes 102400 | tf_op jit(solution)/shard_map/psum | solution.py:21
  123.9 0.0 copy-start
  123.9 0.2 convolution_multiply_fusion
  124.1 3.1 %fusion = f32[56,512]{1,0:T(8,128)S(1)} fusion(f32[100,512]{1,0:T(8,128)S(1)} %convolution_multiply_fusion), kind=kCustom, calls=%all-reduce-scatter | all-reduce-scatter fusion | flops 57345 | bytes 320000
  127.1 2.3 %collective-permute-start = (f32[6,512]{1,0:T(8,128)S(1)}, f32[6,512]{1,0:T(8,128)S(1)}, u32[]{:S(2)}, u32[]{:S(2)}) collective-permute-start(f32[6,512]{1,0:T(8,128)S(1)} %slice), channel_id=1, source_target_pairs={{0,1},{2,3},{4,5},{6,7},{8,9},{10,11},{12,13},{14,15},{16,17},{18,... | collective-permute-start | bytes 36872
  129.4 0.0 copy-done.2
  129.4 0.6 dynamic-slice.4
  130.7 0.0 collective-permute-done
  130.7 0.2 concatenate
  130.9 0.7 constant_dynamic-slice_fusion
  131.5 0.0 copy-done
  (2 shorter events, 0.0 us)
Async XLA Ops:
  7.2 7.3 %copy-start.1 = (s32[512]{0:T(512)S(1)}, s32[512]{0:T(512)}, u32[]{:S(2)}) copy-start(s32[512]{0:T(512)} %param.8) | copy-start | bytes 6148
  7.2 27.3 %all-gather.2.cloned.1.call-start = ((), (), s32[]{:S(2)}) async-start(), calls=%async_computation | async-start | bytes 9830400 | tf_op jit(solution)/shard_map/all_gather | solution.py:16
  19.5 109.9 %copy-start.2 = (u32[32]{0:T(128)S(1)}, u32[32]{0:T(128)}, u32[]{:S(2)}) copy-start(u32[32]{0:T(128)} %constant.18) | copy-start | bytes 388
  123.9 7.6 %copy-start = (f32[128,100]{0,1:T(8,128)}, f32[128,100]{0,1:T(8,128)S(1)}, u32[]{:S(2)}) copy-start(f32[128,100]{0,1:T(8,128)S(1)} %psum.7) | copy-start | bytes 153604
  127.1 3.5 %collective-permute-start = (f32[6,512]{1,0:T(8,128)S(1)}, f32[6,512]{1,0:T(8,128)S(1)}, u32[]{:S(2)}, u32[]{:S(2)}) collective-permute-start(f32[6,512]{1,0:T(8,128)S(1)} %slice), channel_id=1, source_target_pairs={{0,1},{2,3},{4,5},{6,7},{8,9},{10,11},{12,13},{14,15},{16,17},{18,... | collective-permute-start | bytes 36872
Sparse Core Ops, SparseCore 0:
  14.6 19.8 all-gather.1
where the time goes:
time: 139 us; the launch traced here: 138 us
  blocking collectives  80.2 us (58%)
  waiting for transfers between devices  15 us (11%)
  between operations  14.8 us (11%)
  matrix products  12.4 us (9%)
  other arithmetic  11 us (8%)
  local copies, waits for them, and re-layouts  2.69 us (2%)
  starting transfers between devices  2.3 us (2%)
    psum x1, blocking collectives, shards(): pcs = lax.psum(partial_value, 'cell')  77.1 us
    all_gather x1, waiting for transfers between devices, shards(): piece = lax.all_gather(weighted, 'win', axis=0, tiled=True)  15 us
    dot_general x1, matrix products, shards(): lax.dot_general(flat_data, flat_piece, (((1,), (1,)), ((), ())), preferre...  12.3 us
    reduce_sum x1, other arithmetic, shards(): jnp.sum(anomalies.astype(jnp.float32) * mask[None], axis=1)  5.01 us
    convert_element_type x1, other arithmetic, shards(): (eofs.astype(jnp.float32) * (cell_area[None, :] * mask)[None]).astype(jnp...  4.6 us
    unnamed x1, blocking collectives  3.06 us
  transfers between devices with their start and end apart: 2, of which 1 were waited for; matrix products, arithmetic and copies ran while one was open for 4% of the time, Pallas kernels for 0%

commit v1 on v0

--- a/solution.py
+++ b/solution.py
@@ -2,6 +2,14 @@
 import jax.numpy as jnp
 from jax import lax
 from jax.sharding import PartitionSpec as P
+
+
+def added_up(array, axis):
+    devices, total = (lax.axis_size(axis), array)
+    for stride in [1 << k for k in range(devices.bit_length() - 1)]:
+        route = [(i, i ^ stride) for i in range(devices)]
+        total = total + lax.ppermute(total, axis, route)
+    return total
 
 
 def shards(anomalies, eofs, cell_area, levels, counts):
@@ -18,7 +26,7 @@
     partial_value = lax.dot_general(
         flat_data, flat_piece, (((1,), (1,)), ((), ())), preferred_element_type=jnp.float32
     )
-    pcs = lax.psum(partial_value, "cell")
+    pcs = added_up(partial_value, "cell")
     column = jnp.sum(anomalies.astype(jnp.float32) * mask[None], axis=1).astype(jnp.bfloat16)
     pcs_rounded = pcs.astype(jnp.bfloat16)
     windows = lax.axis_size("win")

time: 139 us -> 82.5 us (0.59)
  blocking collectives: 80.2 us -> 3.06 us
  waiting for transfers between devices: 15 us -> 27.2 us
  starting transfers between devices: 2.3 us -> 11 us
    psum x1 -> x0, blocking collectives: 77.1 us -> none  [shards(): pcs = lax.psum(partial_value, 'cell')]
    ppermute x0 -> x4, starting transfers between devices: none -> 8.68 us  [added_up(): total = total + lax.ppermute(total, axis, route)]
    ppermute x0 -> x4, waiting for transfers between devices: none -> 7.14 us  [added_up(): total = total + lax.ppermute(total, axis, route)]
    all_gather x1, waiting for transfers between devices: 15 us -> 20 us  [shards(): piece = lax.all_gather(weighted, 'win', axis=0, tiled=True)]
  transfers between devices with their start and end apart: 2 -> 6, of which waited for: 1 -> 4; matrix products, arithmetic and copies ran while one was open for 4% -> 7% of each run, Pallas kernels for 0% -> 0%
where the time goes in v1:
time: 82.5 us; the launch traced here: 82.2 us
  waiting for transfers between devices  27.2 us (33%)
  between operations  14.8 us (18%)
  matrix products  12.4 us (15%)
  starting transfers between devices  11 us (13%)
  other arithmetic  11 us (13%)
  blocking collectives  3.06 us (4%)
  local copies, waits for them, and re-layouts  2.69 us (3%)
    all_gather x1, waiting for transfers between devices, shards(): piece = lax.all_gather(weighted, 'win', axis=0, tiled=True)  20 us
    dot_general x1, matrix products, shards(): lax.dot_general(flat_data, flat_piece, (((1,), (1,)), ((), ())), preferre...  12.3 us
    ppermute x4, starting transfers between devices, added_up(): total = total + lax.ppermute(total, axis, route)  8.68 us
    ppermute x4, waiting for transfers between devices, added_up(): total = total + lax.ppermute(total, axis, route)  7.14 us
    reduce_sum x1, other arithmetic, shards(): jnp.sum(anomalies.astype(jnp.float32) * mask[None], axis=1)  5 us
    convert_element_type x1, other arithmetic, shards(): (eofs.astype(jnp.float32) * (cell_area[None, :] * mask)[None]).astype(jnp...  4.6 us
    unnamed x1, blocking collectives  3.06 us
    unnamed x1, starting transfers between devices  2.26 us
  transfers between devices with their start and end apart: 6, of which 4 were waited for; matrix products, arithmetic and copies ran while one was open for 7% of the time, Pallas kernels for 0%

profile of v1, /device:TPU:0, one launch (start us, length us, event | category | flops | bytes accessed | tf_op | source)
XLA Modules:
  0.0 82.2 jit_solution(15157126811846779050)
XLA Ops:
  7.2 0.0 all-gather.2.cloned.1.call-start
  7.2 1.2 %dynamic_slice.3 = s32[1]{0:T(128)} dynamic-slice(s32[16]{0:T(128)} %param.9, s32[]{:T(128)S(6)} %select_n.3), dynamic_slice_sizes={1} | dynamic-slice | bytes 12 | tf_op jit(solution)/shard_map/dynamic_slice | solution.py:18
  8.5 0.6 iota_compare_fusion.1
  9.1 0.7 fusion.9
  9.8 4.6 %multiply_convert_fusion = bf16[50,60,512]{2,1,0:T(8,128)(2,1)} fusion(bf16[50,60,512]{2,1,0:T(8,128)(2,1)} %param.6, f32[60,512]{1,0:T(8,128)S(1)} %fusion.9), kind=kLoop, calls=%fused_computation.1 | loop fusion | flops 4608000 | bytes 6266880 | tf_op jit(solution)/shard_map/convert_element_type | solution.py:22
  14.4 0.0 all-gather.2.cloned.1.call-update
  14.5 0.0 copy-start.1
  14.5 20.0 %all-gather.2.cloned.1.call-done = bf16[100,60,512]{2,1,0:T(8,128)(2,1)} async-done(((bf16[50,60,512]{2,1,0:T(8,128)(2,1)}), bf16[100,60,512]{2,1,0:T(8,128)(2,1)}) %all-gather.2.cloned.1.call-update) | async-done | bytes 6144016 | tf_op jit(solution)/shard_map/all_gather | solution.py:24
  34.5 12.3 %fusion.3 = f32[128,100]{0,1:T(8,128)S(1)} fusion(bf16[128,60,512]{2,0,1:T(8,128)(2,1)} %param.5, bf16[100,60,512]{2,1,0:T(8,128)(2,1)} %all-gather.2.cloned.1.call-done), kind=kOutput, calls=%fused_computation.5 | convolution fusion | flops 786432000 | bytes 14059520 | tf_op jit(solution)/shard_map/dot_general | solution.py:26
  46.8 0.0 copy-start.2
  46.8 1.8 %collective-permute-start = (f32[128,100]{0,1:T(8,128)S(1)}, f32[128,100]{0,1:T(8,128)S(1)}, u32[]{:S(2)}, u32[]{:S(2)}) collective-permute-start(f32[128,100]{0,1:T(8,128)S(1)} %fusion.3), channel_id=1, source_target_pairs={{0,2},{2,0},{4,6},{6,4},{8,10},{10,8},{12,14},{14,12},{16,18},{18,... | collective-permute-start | bytes 153608 | tf_op jit(solution)/shard_map/ppermute | solution.py:11
  48.6 2.4 %collective-permute-done = f32[128,100]{0,1:T(8,128)S(1)} collective-permute-done((f32[128,100]{0,1:T(8,128)S(1)}, f32[128,100]{0,1:T(8,128)S(1)}, u32[]{:S(2)}, u32[]{:S(2)}) %collective-permute-start) | collective-permute-done | bytes 51232 | tf_op jit(solution)/shard_map/ppermute | solution.py:11
  51.0 1.8 %collective-permute-start.1 = (f32[128,100]{0,1:T(8,128)S(1)}, f32[128,100]{0,1:T(8,128)S(1)}, u32[]{:S(2)}, u32[]{:S(2)}) collective-permute-start(f32[128,100]{0,1:T(8,128)S(1)} %add.18), channel_id=1, source_target_pairs={{0,4},{2,6},{4,0},{6,2},{8,12},{10,14},{12,8},{14,10},{16,20},{18,... | collective-permute-start | bytes 153608 | tf_op jit(solution)/shard_map/ppermute | solution.py:11
  52.8 2.4 %collective-permute-done.1 = f32[128,100]{0,1:T(8,128)S(1)} collective-permute-done((f32[128,100]{0,1:T(8,128)S(1)}, f32[128,100]{0,1:T(8,128)S(1)}, u32[]{:S(2)}, u32[]{:S(2)}) %collective-permute-start.1) | collective-permute-done | bytes 51232 | tf_op jit(solution)/shard_map/ppermute | solution.py:11
  55.2 1.8 %collective-permute-start.2 = (f32[128,100]{0,1:T(8,128)S(1)}, f32[128,100]{0,1:T(8,128)S(1)}, u32[]{:S(2)}, u32[]{:S(2)}) collective-permute-start(f32[128,100]{0,1:T(8,128)S(1)} %add.19), channel_id=1, source_target_pairs={{0,8},{2,10},{4,12},{6,14},{8,0},{10,2},{12,4},{14,6},{16,24},{18,... | collective-permute-start | bytes 153608 | tf_op jit(solution)/shard_map/ppermute | solution.py:11
  57.0 0.0 copy-done.1
  57.0 2.4 %collective-permute-done.2 = f32[128,100]{0,1:T(8,128)S(1)} collective-permute-done((f32[128,100]{0,1:T(8,128)S(1)}, f32[128,100]{0,1:T(8,128)S(1)}, u32[]{:S(2)}, u32[]{:S(2)}) %collective-permute-start.2) | collective-permute-done | bytes 51232 | tf_op jit(solution)/shard_map/ppermute | solution.py:11
  59.4 3.3 %collective-permute-start.3 = (f32[128,100]{0,1:T(8,128)S(1)}, f32[128,100]{0,1:T(8,128)S(1)}, u32[]{:S(2)}, u32[]{:S(2)}) collective-permute-start(f32[128,100]{0,1:T(8,128)S(1)} %add.20), channel_id=1, source_target_pairs={{0,16},{2,18},{4,20},{6,22},{8,24},{10,26},{12,28},{14,30},{16,0},... | collective-permute-start | bytes 153608 | tf_op jit(solution)/shard_map/ppermute | solution.py:11
  62.7 5.0 %multiply_reduce_fusion = bf16[128,512]{1,0:T(8,128)(2,1)S(1)} fusion(bf16[128,60,512]{2,0,1:T(8,128)(2,1)} %param.5, f32[60,512]{1,0:T(8,128)S(1)} %fusion.8), kind=kLoop, calls=%fused_computation | loop fusion | flops 11730944 | bytes 8118272 | tf_op jit(solution)/shard_map/reduce_sum | solution.py:30
  67.7 0.0 collective-permute-done.3
  67.7 0.0 copy-start
  67.7 0.2 convolution_multiply_fusion
  67.9 3.1 %fusion = f32[56,512]{1,0:T(8,128)S(1)} fusion(f32[100,512]{1,0:T(8,128)S(1)} %convolution_multiply_fusion), kind=kCustom, calls=%all-reduce-scatter | all-reduce-scatter fusion | flops 57345 | bytes 320000
  71.0 2.3 %collective-permute-start.4 = (f32[6,512]{1,0:T(8,128)S(1)}, f32[6,512]{1,0:T(8,128)S(1)}, u32[]{:S(2)}, u32[]{:S(2)}) collective-permute-start(f32[6,512]{1,0:T(8,128)S(1)} %slice), channel_id=1, source_target_pairs={{0,1},{2,3},{4,5},{6,7},{8,9},{10,11},{12,13},{14,15},{16,17},{18,... | collective-permute-start | bytes 36872
  73.2 0.0 copy-done.2
  73.2 0.6 dynamic-slice.4
  74.5 0.0 collective-permute-done.4
  74.5 0.2 concatenate
  74.7 0.7 constant_dynamic-slice_fusion
  75.3 0.0 copy-done
  (6 shorter events, 0.1 us)
Async XLA Ops:
  7.2 27.3 %all-gather.2.cloned.1.call-start = ((), (), s32[]{:S(2)}) async-start(), calls=%async_computation | async-start | bytes 9830400 | tf_op jit(solution)/shard_map/all_gather | solution.py:24
  14.5 42.5 %copy-start.1 = (s32[512]{0:T(512)S(1)}, s32[512]{0:T(512)}, u32[]{:S(2)}) copy-start(s32[512]{0:T(512)} %param.8) | copy-start | bytes 6148
  46.8 26.5 %copy-start.2 = (u32[32]{0:T(128)S(1)}, u32[32]{0:T(128)}, u32[]{:S(2)}) copy-start(u32[32]{0:T(128)} %constant.18) | copy-start | bytes 388
  46.8 4.2 %collective-permute-start = (f32[128,100]{0,1:T(8,128)S(1)}, f32[128,100]{0,1:T(8,128)S(1)}, u32[]{:S(2)}, u32[]{:S(2)}) collective-permute-start(f32[128,100]{0,1:T(8,128)S(1)} %fusion.3), channel_id=1, source_target_pairs={{0,2},{2,0},{4,6},{6,4},{8,10},{10,8},{12,14},{14,12},{16,18},{18,... | collective-permute-start | bytes 153608 | tf_op jit(solution)/shard_map/ppermute | solution.py:11
  51.0 4.2 %collective-permute-start.1 = (f32[128,100]{0,1:T(8,128)S(1)}, f32[128,100]{0,1:T(8,128)S(1)}, u32[]{:S(2)}, u32[]{:S(2)}) collective-permute-start(f32[128,100]{0,1:T(8,128)S(1)} %add.18), channel_id=1, source_target_pairs={{0,4},{2,6},{4,0},{6,2},{8,12},{10,14},{12,8},{14,10},{16,20},{18,... | collective-permute-start | bytes 153608 | tf_op jit(solution)/shard_map/ppermute | solution.py:11
  55.2 4.2 %collective-permute-start.2 = (f32[128,100]{0,1:T(8,128)S(1)}, f32[128,100]{0,1:T(8,128)S(1)}, u32[]{:S(2)}, u32[]{:S(2)}) collective-permute-start(f32[128,100]{0,1:T(8,128)S(1)} %add.19), channel_id=1, source_target_pairs={{0,8},{2,10},{4,12},{6,14},{8,0},{10,2},{12,4},{14,6},{16,24},{18,... | collective-permute-start | bytes 153608 | tf_op jit(solution)/shard_map/ppermute | solution.py:11
  59.4 8.3 %collective-permute-start.3 = (f32[128,100]{0,1:T(8,128)S(1)}, f32[128,100]{0,1:T(8,128)S(1)}, u32[]{:S(2)}, u32[]{:S(2)}) collective-permute-start(f32[128,100]{0,1:T(8,128)S(1)} %add.20), channel_id=1, source_target_pairs={{0,16},{2,18},{4,20},{6,22},{8,24},{10,26},{12,28},{14,30},{16,0},... | collective-permute-start | bytes 153608 | tf_op jit(solution)/shard_map/ppermute | solution.py:11
  67.7 7.6 %copy-start = (f32[128,100]{0,1:T(8,128)}, f32[128,100]{0,1:T(8,128)S(1)}, u32[]{:S(2)}) copy-start(f32[128,100]{0,1:T(8,128)S(1)} %add.21) | copy-start | bytes 153604
  71.0 3.5 %collective-permute-start.4 = (f32[6,512]{1,0:T(8,128)S(1)}, f32[6,512]{1,0:T(8,128)S(1)}, u32[]{:S(2)}, u32[]{:S(2)}) collective-permute-start(f32[6,512]{1,0:T(8,128)S(1)} %slice), channel_id=1, source_target_pairs={{0,1},{2,3},{4,5},{6,7},{8,9},{10,11},{12,13},{14,15},{16,17},{18,... | collective-permute-start | bytes 36872
Sparse Core Ops, SparseCore 0:
  14.6 19.8 all-gather.1
